TPU v7x, 32 devices: a whole 2x2x4 slice. The times are simulated.
32 devices in a mesh: comp: 8 (over y, x, core), strip: 4 (over z).
Axes of the slice: x: 2, y: 2, z: 4, core: 2. Of those that a mesh axis runs over, the one named last changes fastest.
Arguments:
- energy: bfloat16 [1152, 64, 512], P('comp', 'strip'), may hold values from 0.049804688 to 2
- heading: float32 [1152], P('comp'), may hold values from -3.140625 to 3.140625
- growth: float32 [1152], P('comp'), may hold values from 0.005 to 0.05
- courant: float32 [1152, 2], P('comp'), may hold values from -0.45 to 0.45
- dissip: float32 [1152], replicated, may hold values from 0.05 to 0.5
- mixing: bfloat16 [1152, 1152], replicated, may hold values from -0.1875 to 0.1875
- transfer: bfloat16 [1152, 1152], replicated, may hold values from -0.046875 to 0.046875
- pattern: int32 [1152], replicated, may hold values from 0 to 1151, each once
- regime_winds: float32 [8, 2], replicated, may hold values from -8 to 8
- regime: int32 [32, 32], P('strip'), may hold values from 0 to 7
- seeds: int32 [32, 32], P('strip'), may hold values from 0 to 1023
- sea_mask: int32 [64, 512], P('strip'), may hold values 0 or 1
Outputs:
- energy_out: float32 [1152, 64, 512], P('comp', 'strip')
Inputs may be any that keep to these rules, and one draw needn't show every extreme that they name: `pattern`: each component is named exactly once.
All inputs are finite; a program needn't handle non-finite values. No bound on the sum of `sea_mask` on one device may be relied on, other than what follows from the above.
Results may differ from a plain program's by a relative error of at most 0.0008.
Values may be sent and summed in bfloat16 or wider, within the bound.
No kernel may reach another device: no remote copies, remote signals or barrier semaphores. Data moves between devices by JAX's collectives and lax.ppermute only.
A program may use at most 192 MiB of HBM per device.

v0:
```python
import jax
import jax.numpy as jnp
from jax import lax
from jax.sharding import PartitionSpec as P

SUBSTEPS = 4
TILE_ROWS = 2
TILE_COLS = 16


def with_halo(block, sides, width):
    for axis, dim in sides:
        count = lax.axis_size(axis)
        forward = [(i, i + 1) for i in range(count - 1)]
        backward = [(target, source) for source, target in forward]
        low = lax.ppermute(
            lax.slice_in_dim(block, block.shape[dim] - width, None, axis=dim), axis, forward
        )
        high = lax.ppermute(lax.slice_in_dim(block, 0, width, axis=dim), axis, backward)
        block = jnp.concatenate([low, block, high], axis=dim)
    return block


def strip_winds(regime_winds, regime, seeds):
    levels = jnp.arange(regime_winds.shape[0], dtype=jnp.int32)
    onehot = (regime[..., None] == levels).astype(jnp.float32)
    base_u = jnp.sum(onehot * regime_winds[:, 0], axis=-1)
    base_v = jnp.sum(onehot * regime_winds[:, 1], axis=-1)
    tile_u = base_u + 0.25 * (seeds % 13 - 6).astype(jnp.float32)
    tile_v = base_v + 0.4 * (seeds % 7 - 3).astype(jnp.float32)
    wind_u = jnp.repeat(jnp.repeat(tile_u, TILE_ROWS, axis=0), TILE_COLS, axis=1)
    wind_v = jnp.repeat(jnp.repeat(tile_v, TILE_ROWS, axis=0), TILE_COLS, axis=1)
    return (wind_u, wind_v)


def cell_terms(spectra, mixing, transfer, pattern, dissip):
    spectrum_shape = spectra.shape
    flattened = spectra.reshape(spectrum_shape[0], -1)
    mixed_terms = jnp.dot(mixing, flattened, preferred_element_type=jnp.float32)
    partner = jnp.take(flattened, pattern, axis=0)
    product = (mixed_terms * partner.astype(jnp.float32)).astype(jnp.bfloat16)
    nonlinear = jnp.dot(transfer, product, preferred_element_type=jnp.float32)
    widened = flattened.astype(jnp.float32)
    mean_energy = jnp.sum(widened, axis=0) / spectrum_shape[0]
    result = nonlinear - dissip[:, None] * mean_energy[None, :] * widened
    return result.astype(jnp.bfloat16).reshape(spectrum_shape)


def advect(padded, sea_field, courant_x, courant_y):
    flux_y = (
        jnp.maximum(courant_y, 0.0) * padded[..., :-1, :]
        + jnp.minimum(courant_y, 0.0) * padded[..., 1:, :]
    )
    center = padded[..., 1:-1, :]
    widths = [(0, 0)] * (center.ndim - 1) + [(1, 1)]
    padded_x = jnp.pad(center, widths)
    flux_x = (
        jnp.maximum(courant_x, 0.0) * padded_x[..., :-1]
        + jnp.minimum(courant_x, 0.0) * padded_x[..., 1:]
    )
    return (
        center - (flux_x[..., 1:] - flux_x[..., :-1]) - (flux_y[..., 1:, :] - flux_y[..., :-1, :])
    ) * sea_field


def per_device(
    energy,
    heading,
    growth,
    courant,
    dissip,
    mixing,
    transfer,
    pattern,
    regime_winds,
    regime,
    seeds,
    sea_mask,
):
    wind_u, wind_v = strip_winds(regime_winds, regime, seeds)
    widened = energy.astype(jnp.float32)
    drive = (
        wind_u[None] * jnp.cos(heading)[:, None, None]
        + wind_v[None] * jnp.sin(heading)[:, None, None]
    )
    input_term = growth[:, None, None] * jnp.maximum(0.0, drive) * widened
    returned = lax.all_to_all(
        cell_terms(
            lax.all_to_all(energy, "comp", split_axis=1, concat_axis=0, tiled=True),
            mixing,
            transfer,
            pattern,
            dissip,
        ),
        "comp",
        split_axis=0,
        concat_axis=1,
        tiled=True,
    )
    energy_field = widened + input_term + returned.astype(jnp.float32)
    sea_field = sea_mask.astype(jnp.float32)
    courant_x = courant[:, 0][:, None, None]
    courant_y = courant[:, 1][:, None, None]
    for substep in range(SUBSTEPS):
        padded = with_halo(energy_field, (("strip", 1),), 1)
        energy_field = advect(padded, sea_field, courant_x, courant_y)
    return energy_field


def solution(mesh):
    placed = (
        P("comp", "strip", None),
        P("comp"),
        P("comp"),
        P("comp", None),
        P(),
        P(),
        P(),
        P(),
        P(),
        P("strip", None),
        P("strip", None),
        P("strip", None),
    )
    return jax.shard_map(
        per_device, mesh=mesh, in_specs=placed, out_specs=P("comp", "strip", None), check_vma=False
    )
```

profile of v0, /device:TPU:26, one launch (start us, length us, event | category | flops | bytes accessed | tf_op | source)
XLA Modules:
  0.0 194.6 jit_solution(15152616332735893977)
XLA Ops:
  0.0 4.5 %copy.33 = bf16[144,16,512]{2,0,1:T(8,128)(2,1)} copy(bf16[144,16,512]{2,1,0:T(8,128)(2,1)} %param.12) | data formatting | bytes 4718592 | tf_op args[0]
  4.5 4.8 %all-to-all-start = ((bf16[144,16,512]{2,0,1:T(8,128)(2,1)}), bf16[144,16,512]{2,0,1:T(8,128)(2,1)}, u32[]{:S(2)}, u32[]{:S(2)}) async-start(bf16[144,16,512]{2,0,1:T(8,128)(2,1)} %copy.33), calls=%async_computation | async-start | bytes 4718592 | tf_op jit(solution)/shard_map/all_to_all | solution.py:89
  9.4 28.0 %all-to-all-done = bf16[144,16,512]{2,0,1:T(8,128)(2,1)} async-done(((bf16[144,16,512]{2,0,1:T(8,128)(2,1)}), bf16[144,16,512]{2,0,1:T(8,128)(2,1)}, u32[]{:S(2)}, u32[]{:S(2)}) %all-to-all-start) | async-done | bytes 2359328 | tf_op jit(solution)/shard_map/all_to_all | solution.py:89
  37.4 4.2 %convert_reduce_fusion = f32[2,512]{1,0:T(2,128)S(1)} fusion(bf16[144,8,2,512]{3,0,2,1:T(8,128)(2,1)} %bitcast.4), kind=kLoop, calls=%fused_computation.59 | loop fusion | flops 2358272 | bytes 2363392 | tf_op jit(solution)/shard_map/reduce_sum | solution.py:44
  41.6 4.1 %copy.35 = bf16[144,8,2,512]{3,2,0,1:T(2,128)(2,1)S(1)} copy(bf16[144,8,2,512]{3,0,2,1:T(8,128)(2,1)} %bitcast.4) | data formatting | bytes 4718592 | tf_op jit(solution)/shard_map/all_to_all | solution.py:89
  47.7 4.4 %copy.36 = bf16[1152,1024]{0,1:T(8,128)(2,1)} copy(bf16[1152,1024]{1,0:T(8,128)(2,1)} %bitcast.33) | data formatting | bytes 4718592 | tf_op jit(solution)/shard_map/reshape | solution.py:38
  52.1 8.6 %gather_fusion = bf16[1152,1024]{1,0:T(8,128)(2,1)} fusion(bf16[1152,1024]{1,0:T(8,128)(2,1)} %bitcast.34, s32[2048]{0:T(1024)S(1)} %pad_clamp_fusion), kind=kCustom, calls=%fused_computation | custom fusion | bytes 4723200 | tf_op jit(solution)/shard_map/jit(_take)/gather | solution.py:40
  60.7 12.2 %fusion.29 = bf16[1152,1024]{0,1:T(8,128)(2,1)} fusion(bf16[1152,1024]{0,1:T(8,128)(2,1)} %copy.36, bf16[1152,1152]{1,0:T(8,128)(2,1)S(1)} %copy-done, f32[1024]{0:T(1024)S(1)} %bitcast.57, f32[1152]{0:T(1024)S(1)} %copy-done.11, bf16[1152,1152]{1,0:T(8,128)(2,1)} %param.17, bf16[1152,1024]{1,0:T(8,128)(2,1)} %bitcast.35, ...), kind=kOutput, calls=%fused_computation.58 | convolution fusion | flops 5446434816 | bytes 14755456 | tf_op jit(solution)/shard_map/dot_general | solution.py:42
  72.9 6.8 %copy.37 = bf16[1152,2,512]{2,1,0:T(2,128)(2,1)} copy(bf16[1152,2,512]{0,2,1:T(8,128)(2,1)} %bitcast.38) | data formatting | bytes 4718592 | tf_op jit(solution)/shard_map/reshape | solution.py:46
  79.7 5.8 %all-to-all-start.1 = ((bf16[1152,2,512]{2,1,0:T(2,128)(2,1)}), bf16[1152,2,512]{2,1,0:T(2,128)(2,1)}, u32[]{:S(2)}, u32[]{:S(2)}) async-start(bf16[1152,2,512]{2,1,0:T(2,128)(2,1)} %copy.37), calls=%async_computation.1 | async-start | bytes 4718592 | tf_op jit(solution)/shard_map/all_to_all | solution.py:87
  86.3 27.2 %all-to-all-done.1 = bf16[1152,2,512]{2,1,0:T(2,128)(2,1)} async-done(((bf16[1152,2,512]{2,1,0:T(2,128)(2,1)}), bf16[1152,2,512]{2,1,0:T(2,128)(2,1)}, u32[]{:S(2)}, u32[]{:S(2)}) %all-to-all-start.1) | async-done | bytes 2359328 | tf_op jit(solution)/shard_map/all_to_all | solution.py:87
  125.9 3.3 %collective-permute-done.1 = f32[144,1,512]{2,0,1:T(8,128)S(1)} collective-permute-done((f32[144,1,512]{2,0,1:T(8,128)S(1)}, f32[144,1,512]{2,0,1:T(8,128)S(1)}, u32[]{:S(2)}, u32[]{:S(2)}) %collective-permute-start.1) | collective-permute-done | bytes 294944 | tf_op jit(solution)/shard_map/ppermute | solution.py:19
  129.2 4.1 %collective-permute-done = f32[144,1,512]{2,0,1:T(8,128)S(1)} collective-permute-done((f32[144,1,512]{2,0,1:T(8,128)S(1)}, f32[144,1,512]{2,0,1:T(8,128)S(1)}, u32[]{:S(2)}, u32[]{:S(2)}) %collective-permute-start) | collective-permute-done | bytes 294944 | tf_op jit(solution)/shard_map/ppermute | solution.py:16
  141.0 3.6 %fusion.4 = f32[144,16,513]{2,0,1:T(8,128)} fusion(f32[144,16,512]{2,0,1:T(8,128)S(1)} %fusion.27, f32[144]{0:T(256)S(1)} %bitcast.54, f32[144]{0:T(256)S(1)} %bitcast.50), kind=kLoop, calls=%fused_computation.14 | loop fusion | flops 3545856 | bytes 9447552 | tf_op jit(solution)/shard_map/add | solution.py:58
  145.0 4.1 %collective-permute-done.2 = f32[144,1,512]{2,0,1:T(8,128)S(1)} collective-permute-done((f32[144,1,512]{2,0,1:T(8,128)S(1)}, f32[144,1,512]{2,0,1:T(8,128)S(1)}, u32[]{:S(2)}, u32[]{:S(2)}) %collective-permute-start.2) | collective-permute-done | bytes 294944 | tf_op jit(solution)/shard_map/ppermute | solution.py:16
  150.7 5.5 %fusion.24 = f32[144,16,512]{2,0,1:T(8,128)S(1)} fusion(f32[144,17,512]{2,0,1:T(8,128)S(1)} %fusion.13, f32[144,16,512]{2,0,1:T(8,128)S(1)} %fusion.27, f32[144,16,513]{2,0,1:T(8,128)} %fusion.4, f32[16,512]{1,0:T(8,128)S(1)} %convert_element_type.57), kind=kLoop, calls=%fused_computation.48 | loop fusion | flops 5898240 | bytes 28344320 | tf_op jit(solution)/shard_map/mul | solution.py:61
  156.3 2.5 %collective-permute-start.5 = (f32[144,1,512]{2,0,1:T(8,128)S(1)}, f32[144,1,512]{2,0,1:T(8,128)S(1)}, u32[]{:S(2)}, u32[]{:S(2)}) collective-permute-start(f32[144,1,512]{2,0,1:T(8,128)S(1)} %get-tuple-element.9), channel_id=1, source_target_pairs={{1,0},{2,1},{3,2},{5,4},{6,5},{7,6},{9,8},{10,9},{11,10},{13,12},{... | collective-permute-start | bytes 884744 | tf_op jit(solution)/shard_map/ppermute | solution.py:19
  160.3 3.6 %fusion.7 = f32[144,16,513]{2,0,1:T(8,128)} fusion(f32[144,16,512]{2,0,1:T(8,128)S(1)} %fusion.24, f32[144]{0:T(256)S(1)} %bitcast.55, f32[144]{0:T(256)S(1)} %bitcast.51), kind=kLoop, calls=%fused_computation.17 | loop fusion | flops 3545856 | bytes 9447552 | tf_op jit(solution)/shard_map/add | solution.py:58
  164.0 3.5 %collective-permute-done.4 = f32[144,1,512]{2,0,1:T(8,128)S(1)} collective-permute-done((f32[144,1,512]{2,0,1:T(8,128)S(1)}, f32[144,1,512]{2,0,1:T(8,128)S(1)}, u32[]{:S(2)}, u32[]{:S(2)}) %collective-permute-start.4) | collective-permute-done | bytes 294944 | tf_op jit(solution)/shard_map/ppermute | solution.py:16
  169.0 5.5 %fusion.21 = f32[144,16,512]{2,0,1:T(8,128)S(1)} fusion(f32[144,17,512]{2,0,1:T(8,128)S(1)} %fusion.14, f32[144,16,512]{2,0,1:T(8,128)S(1)} %fusion.24, f32[144,16,513]{2,0,1:T(8,128)} %fusion.7, f32[16,512]{1,0:T(8,128)S(1)} %convert_element_type.57), kind=kLoop, calls=%fused_computation.43 | loop fusion | flops 5898240 | bytes 28344320 | tf_op jit(solution)/shard_map/mul | solution.py:61
  174.6 2.4 %collective-permute-start.7 = (f32[144,1,512]{2,0,1:T(8,128)S(1)}, f32[144,1,512]{2,0,1:T(8,128)S(1)}, u32[]{:S(2)}, u32[]{:S(2)}) collective-permute-start(f32[144,1,512]{2,0,1:T(8,128)S(1)} %get-tuple-element.7), channel_id=1, source_target_pairs={{1,0},{2,1},{3,2},{5,4},{6,5},{7,6},{9,8},{10,9},{11,10},{13,12},{... | collective-permute-start | bytes 884744 | tf_op jit(solution)/shard_map/ppermute | solution.py:19
  181.2 4.4 %collective-permute-done.6 = f32[144,1,512]{2,0,1:T(8,128)S(1)} collective-permute-done((f32[144,1,512]{2,0,1:T(8,128)S(1)}, f32[144,1,512]{2,0,1:T(8,128)S(1)}, u32[]{:S(2)}, u32[]{:S(2)}) %collective-permute-start.6) | collective-permute-done | bytes 294944 | tf_op jit(solution)/shard_map/ppermute | solution.py:16
  187.2 2.5 %fusion.18 = f32[144,16,512]{2,0,1:T(8,128)S(1)} fusion(f32[144,17,512]{2,0,1:T(8,128)S(1)} %fusion.15, f32[144,16,512]{2,0,1:T(8,128)S(1)} %fusion.21, f32[144,16,513]{2,0,1:T(8,128)S(1)} %fusion.10, f32[16,512]{1,0:T(8,128)S(1)} %convert_element_type.57), kind=kLoop, calls=%fused_computation.38 | loop fusion | flops 5898240 | bytes 28344320 | tf_op jit(solution)/shard_map/mul | solution.py:61
  189.6 4.9 %copy.40 = f32[144,16,512]{2,1,0:T(8,128)} copy(f32[144,16,512]{2,0,1:T(8,128)S(1)} %fusion.18) | data formatting | bytes 9437184 | tf_op jit(solution)/shard_map/mul | solution.py:61
  (66 shorter events, 33.6 us)
Async XLA Ops:
  0.0 60.7 %copy-start = (bf16[1152,1152]{1,0:T(8,128)(2,1)S(1)}, bf16[1152,1152]{1,0:T(8,128)(2,1)}, u32[]{:S(2)}) copy-start(bf16[1152,1152]{1,0:T(8,128)(2,1)} %param.18) | copy-start | bytes 7962628
  0.0 9.3 %copy-start.3 = (s32[1152]{0:T(1024)S(1)}, s32[1152]{0:T(1024)}, u32[]{:S(2)}) copy-start(s32[1152]{0:T(1024)} %param.19) | copy-start | bytes 13828
  4.5 32.9 %all-to-all-start = ((bf16[144,16,512]{2,0,1:T(8,128)(2,1)}), bf16[144,16,512]{2,0,1:T(8,128)(2,1)}, u32[]{:S(2)}, u32[]{:S(2)}) async-start(bf16[144,16,512]{2,0,1:T(8,128)(2,1)} %copy.33), calls=%async_computation | async-start | bytes 4718592 | tf_op jit(solution)/shard_map/all_to_all | solution.py:89
  52.1 8.6 %copy-start.11 = (f32[1152]{0:T(1024)S(1)}, f32[1152]{0:T(1024)}, u32[]{:S(2)}) copy-start(f32[1152]{0:T(1024)} %param.16) | copy-start | bytes 13828
  72.9 12.6 %copy-start.4 = (s32[16,512]{1,0:T(8,128)S(1)}, s32[16,512]{1,0:T(8,128)}, u32[]{:S(2)}) copy-start(s32[16,512]{1,0:T(8,128)} %param.23) | copy-start | bytes 98308
  72.9 12.7 %copy-start.10 = (f32[8,2]{0,1:T(2,128)S(1)}, f32[8,2]{0,1:T(2,128)}, u32[]{:S(2)}) copy-start(f32[8,2]{0,1:T(2,128)} %param.20) | copy-start | bytes 196
  72.9 12.7 %copy-start.6 = (s32[8,32]{1,0:T(8,128)S(1)}, s32[8,32]{1,0:T(8,128)}, u32[]{:S(2)}) copy-start(s32[8,32]{1,0:T(8,128)} %param.21) | copy-start | bytes 3076
  72.9 12.8 %copy-start.5 = (s32[8,32]{1,0:T(8,128)S(1)}, s32[8,32]{1,0:T(8,128)}, u32[]{:S(2)}) copy-start(s32[8,32]{1,0:T(8,128)} %param.22) | copy-start | bytes 3076
  72.9 13.4 %copy-start.9 = (f32[144]{0:T(256)S(1)}, f32[144]{0:T(256)}, u32[]{:S(2)}) copy-start(f32[144]{0:T(256)} %param.13) | copy-start | bytes 1732
  72.9 13.4 %copy-start.7 = (f32[144,2]{0,1:T(2,128)S(1)}, f32[144,2]{0,1:T(2,128)}, u32[]{:S(2)}) copy-start(f32[144,2]{0,1:T(2,128)} %param.15) | copy-start | bytes 3460
  79.7 33.9 %all-to-all-start.1 = ((bf16[1152,2,512]{2,1,0:T(2,128)(2,1)}), bf16[1152,2,512]{2,1,0:T(2,128)(2,1)}, u32[]{:S(2)}, u32[]{:S(2)}) async-start(bf16[1152,2,512]{2,1,0:T(2,128)(2,1)} %copy.37), calls=%async_computation.1 | async-start | bytes 4718592 | tf_op jit(solution)/shard_map/all_to_all | solution.py:87
  116.3 1.7 copy-start.2
  116.3 1.7 copy-start.8
  120.4 8.8 %collective-permute-start.1 = (f32[144,1,512]{2,0,1:T(8,128)S(1)}, f32[144,1,512]{2,0,1:T(8,128)S(1)}, u32[]{:S(2)}, u32[]{:S(2)}) collective-permute-start(f32[144,1,512]{2,0,1:T(8,128)S(1)} %get-tuple-element.13), channel_id=1, source_target_pairs={{1,0},{2,1},{3,2},{5,4},{6,5},{7,6},{9,8},{10,9},{11,10},{13,12},{... | collective-permute-start | bytes 884744 | tf_op jit(solution)/shard_map/ppermute | solution.py:19
  122.7 10.6 %collective-permute-start = (f32[144,1,512]{2,0,1:T(8,128)S(1)}, f32[144,1,512]{2,0,1:T(8,128)S(1)}, u32[]{:S(2)}, u32[]{:S(2)}) collective-permute-start(f32[144,1,512]{2,0,1:T(8,128)S(1)} %get-tuple-element.14), channel_id=1, source_target_pairs={{0,1},{1,2},{2,3},{4,5},{5,6},{6,7},{8,9},{9,10},{10,11},{12,13},{... | collective-permute-start | bytes 884744 | tf_op jit(solution)/shard_map/ppermute | solution.py:16
  137.3 7.7 %collective-permute-start.3 = (f32[144,1,512]{2,0,1:T(8,128)S(1)}, f32[144,1,512]{2,0,1:T(8,128)S(1)}, u32[]{:S(2)}, u32[]{:S(2)}) collective-permute-start(f32[144,1,512]{2,0,1:T(8,128)S(1)} %get-tuple-element.11), channel_id=1, source_target_pairs={{1,0},{2,1},{3,2},{5,4},{6,5},{7,6},{9,8},{10,9},{11,10},{13,12},{... | collective-permute-start | bytes 884744 | tf_op jit(solution)/shard_map/ppermute | solution.py:19
  139.7 9.4 %collective-permute-start.2 = (f32[144,1,512]{2,0,1:T(8,128)S(1)}, f32[144,1,512]{2,0,1:T(8,128)S(1)}, u32[]{:S(2)}, u32[]{:S(2)}) collective-permute-start(f32[144,1,512]{2,0,1:T(8,128)S(1)} %get-tuple-element.12), channel_id=1, source_target_pairs={{0,1},{1,2},{2,3},{4,5},{5,6},{6,7},{8,9},{9,10},{10,11},{12,13},{... | collective-permute-start | bytes 884744 | tf_op jit(solution)/shard_map/ppermute | solution.py:16
  156.3 7.7 %collective-permute-start.5 = (f32[144,1,512]{2,0,1:T(8,128)S(1)}, f32[144,1,512]{2,0,1:T(8,128)S(1)}, u32[]{:S(2)}, u32[]{:S(2)}) collective-permute-start(f32[144,1,512]{2,0,1:T(8,128)S(1)} %get-tuple-element.9), channel_id=1, source_target_pairs={{1,0},{2,1},{3,2},{5,4},{6,5},{7,6},{9,8},{10,9},{11,10},{13,12},{... | collective-permute-start | bytes 884744 | tf_op jit(solution)/shard_map/ppermute | solution.py:19
  158.8 8.6 %collective-permute-start.4 = (f32[144,1,512]{2,0,1:T(8,128)S(1)}, f32[144,1,512]{2,0,1:T(8,128)S(1)}, u32[]{:S(2)}, u32[]{:S(2)}) collective-permute-start(f32[144,1,512]{2,0,1:T(8,128)S(1)} %get-tuple-element.10), channel_id=1, source_target_pairs={{0,1},{1,2},{2,3},{4,5},{5,6},{6,7},{8,9},{9,10},{10,11},{12,13},{... | collective-permute-start | bytes 884744 | tf_op jit(solution)/shard_map/ppermute | solution.py:16
  174.6 6.6 %collective-permute-start.7 = (f32[144,1,512]{2,0,1:T(8,128)S(1)}, f32[144,1,512]{2,0,1:T(8,128)S(1)}, u32[]{:S(2)}, u32[]{:S(2)}) collective-permute-start(f32[144,1,512]{2,0,1:T(8,128)S(1)} %get-tuple-element.7), channel_id=1, source_target_pairs={{1,0},{2,1},{3,2},{5,4},{6,5},{7,6},{9,8},{10,9},{11,10},{13,12},{... | collective-permute-start | bytes 884744 | tf_op jit(solution)/shard_map/ppermute | solution.py:19
  177.0 8.6 %collective-permute-start.6 = (f32[144,1,512]{2,0,1:T(8,128)S(1)}, f32[144,1,512]{2,0,1:T(8,128)S(1)}, u32[]{:S(2)}, u32[]{:S(2)}) collective-permute-start(f32[144,1,512]{2,0,1:T(8,128)S(1)} %get-tuple-element.8), channel_id=1, source_target_pairs={{0,1},{1,2},{2,3},{4,5},{5,6},{6,7},{8,9},{9,10},{10,11},{12,13},{... | collective-permute-start | bytes 884744 | tf_op jit(solution)/shard_map/ppermute | solution.py:16
  187.2 7.4 %copy-start.1 = (bf16[1152,1152]{1,0:T(8,128)(2,1)S(1)}, bf16[1152,1152]{1,0:T(8,128)(2,1)}, u32[]{:S(2)}) copy-start(bf16[1152,1152]{1,0:T(8,128)(2,1)} %param.18) | copy-start | bytes 7962628
where the time goes:
time: 195 us
  waiting for transfers between devices  76 us (39%)
  other arithmetic  40.5 us (21%)
  local copies, waits for them, and re-layouts  39.9 us (20%)
  starting transfers between devices  25.6 us (13%)
  matrix products  12.2 us (6%)
    all_to_all x1, waiting for transfers between devices, per_device(): lax.all_to_all(energy, 'comp', split_axis=1, concat_axis=0, tiled=True)  28 us
    all_to_all x1, waiting for transfers between devices, per_device(): lax.all_to_all(cell_terms(lax.all_to_all(energy, 'comp', split_axis=1, co...  27.2 us
    ppermute x4, waiting for transfers between devices, with_halo(): lax.ppermute(lax.slice_in_dim(block, block.shape[dim] - width, None, axis...  16.1 us
    mul x4, other arithmetic, advect(): (center - (flux_x[..., 1:] - flux_x[..., :-1]) - (flux_y[..., 1:, :] - fl...  15.9 us
    dot_general x1, matrix products, cell_terms(): nonlinear = jnp.dot(transfer, product, preferred_element_type=jnp.float32)  12.2 us
    add x4, other arithmetic, advect(): jnp.maximum(courant_x, 0.0) * padded_x[..., :-1]  11 us
    ppermute x4, starting transfers between devices, with_halo(): lax.ppermute(lax.slice_in_dim(block, 0, width, axis=dim), axis, backward)  9.67 us
    gather x1, local copies, waits for them, and re-layouts, cell_terms(): partner = jnp.take(flattened, pattern, axis=0)  8.59 us
  transfers between devices with their start and end apart: 10, of which 9 were waited for; matrix products, arithmetic and copies ran while one was open for 6% of the time, Pallas kernels for 0%

commit v1 on v0

--- a/solution.py
+++ b/solution.py
@@ -86,7 +86,15 @@
     input_term = growth[:, None, None] * jnp.maximum(0.0, drive) * widened
     returned = lax.all_to_all(
         cell_terms(
-            lax.all_to_all(energy, "comp", split_axis=1, concat_axis=0, tiled=True),
+            jnp.concatenate(
+                lax.all_to_all(
+                    jnp.stack(jnp.split(energy, lax.axis_size("comp"), axis=1), axis=0),
+                    "comp",
+                    0,
+                    0,
+                ),
+                axis=0,
+            ),
             mixing,
             transfer,
             pattern,

time: 195 us -> 210 us (1.077)
  local copies, waits for them, and re-layouts: 39.9 us -> 55.4 us
    unnamed x27 -> x33, local copies, waits for them, and re-layouts: 7.76 us -> 20.8 us
    another operation x0 -> x2, local copies, waits for them, and re-layouts: none -> 6.6 us  [the longest x1 4.31 us: cell_terms(): flattened = spectra.reshape(spectrum_shape[0], -1)]
    gather x1 -> x2, local copies, waits for them, and re-layouts: 8.59 us -> 13 us  [cell_terms(): partner = jnp.take(flattened, pattern, axis=0)]
    reshape x1 -> x0, local copies, waits for them, and re-layouts: 4.37 us -> none  [cell_terms(): flattened = spectra.reshape(spectrum_shape[0], -1)]
    all_to_all x2 -> x1, local copies, waits for them, and re-layouts: 6.13 us -> 2.04 us  [per_device(): lax.all_to_all(cell_terms(jnp.concatenate(lax.all_to_all(jnp.stack(jnp.sp...]
where the time goes in v1:
time: 210 us; the launch traced here: 209 us
  waiting for transfers between devices  76 us (36%)
  local copies, waits for them, and re-layouts  55.4 us (26%)
  other arithmetic  39.9 us (19%)
  starting transfers between devices  25.6 us (12%)
  matrix products  11.3 us (5%)
    all_to_all x1, waiting for transfers between devices, per_device(): lax.all_to_all(jnp.stack(jnp.split(energy, lax.axis_size('comp'), axis=1)...  28 us
    all_to_all x1, waiting for transfers between devices, per_device(): lax.all_to_all(cell_terms(jnp.concatenate(lax.all_to_all(jnp.stack(jnp.sp...  27.2 us
    unnamed x33, local copies, waits for them, and re-layouts  20.8 us
    ppermute x4, waiting for transfers between devices, with_halo(): lax.ppermute(lax.slice_in_dim(block, block.shape[dim] - width, None, axis...  16.1 us
    mul x4, other arithmetic, advect(): (center - (flux_x[..., 1:] - flux_x[..., :-1]) - (flux_y[..., 1:, :] - fl...  15.9 us
    gather x2, local copies, waits for them, and re-layouts, cell_terms(): partner = jnp.take(flattened, pattern, axis=0)  13 us
    dot_general x1, matrix products, cell_terms(): nonlinear = jnp.dot(transfer, product, preferred_element_type=jnp.float32)  11.3 us
    add x4, other arithmetic, advect(): jnp.maximum(courant_x, 0.0) * padded_x[..., :-1]  11 us
  transfers between devices with their start and end apart: 10, of which 9 were waited for; matrix products, arithmetic and copies ran while one was open for 6% of the time, Pallas kernels for 0%

profile of v1, /device:TPU:26, one launch (start us, length us, event | category | flops | bytes accessed | tf_op | source)
XLA Modules:
  0.0 208.7 jit_solution(8088299828358412936)
XLA Ops:
  18.2 4.8 %all-to-all-start = ((bf16[8,144,2,512]{3,2,1,0:T(2,128)(2,1)}), bf16[8,144,2,512]{3,2,1,0:T(2,128)(2,1)}, u32[]{:S(2)}, u32[]{:S(2)}) async-start(bf16[8,144,2,512]{3,2,1,0:T(2,128)(2,1)} %bitcast_dynamic-update-slice_fusion), calls=%async_computation | async-start | bytes 4718592 | tf_op jit(solution)/shard_map/all_to_all | solution.py:90
  23.0 28.0 %all-to-all-done = bf16[8,144,2,512]{3,2,1,0:T(2,128)(2,1)} async-done(((bf16[8,144,2,512]{3,2,1,0:T(2,128)(2,1)}), bf16[8,144,2,512]{3,2,1,0:T(2,128)(2,1)}, u32[]{:S(2)}, u32[]{:S(2)}) %all-to-all-start) | async-done | bytes 2359328 | tf_op jit(solution)/shard_map/all_to_all | solution.py:90
  51.0 3.7 %convert_reduce_fusion = f32[2,512]{1,0:T(2,128)S(1)} fusion(bf16[8,144,2,512]{3,2,1,0:T(2,128)(2,1)} %all-to-all-done), kind=kLoop, calls=%fused_computation.60 | loop fusion | flops 2358272 | bytes 2363392 | tf_op jit(solution)/shard_map/reduce_sum | solution.py:44
  54.7 3.7 %copy.38 = bf16[144,8,2,512]{3,1,2,0:T(8,128)(2,1)} copy(bf16[144,8,2,512]{3,2,1,0:T(2,128)(2,1)} %bitcast.24) | data formatting | bytes 4718592
  58.4 4.3 %copy.33 = bf16[1152,1024]{0,1:T(8,128)(2,1)} copy(bf16[1152,1024]{1,0:T(8,128)(2,1)} %bitcast.52) | data formatting | bytes 4718592 | tf_op jit(solution)/shard_map/reshape;reshape | solution.py:38
  62.7 8.6 %gather_fusion = bf16[1152,1024]{1,0:T(8,128)(2,1)} fusion(bf16[1152,1024]{1,0:T(8,128)(2,1)} %bitcast.53, s32[2048]{0:T(1024)S(1)} %pad_clamp_fusion), kind=kCustom, calls=%fused_computation | custom fusion | bytes 4723200 | tf_op jit(solution)/shard_map/jit(_take)/gather | solution.py:40
  71.3 4.4 %copy.32 = bf16[1152,1024]{0,1:T(8,128)(2,1)} copy(bf16[1152,1024]{1,0:T(8,128)(2,1)} %gather_fusion) | data formatting | bytes 4718592 | tf_op jit(solution)/shard_map/jit(_take)/gather | solution.py:40
  75.7 11.3 %fusion.29 = bf16[1152,1024]{0,1:T(8,128)(2,1)} fusion(bf16[1152,1024]{0,1:T(8,128)(2,1)} %copy.33, bf16[1152,1152]{1,0:T(8,128)(2,1)S(1)} %copy-done, f32[1024]{0:T(1024)S(1)} %bitcast.75, f32[1152]{0:T(1024)S(1)} %copy-done.11, bf16[1152,1024]{1,0:T(8,128)(2,1)} %bitcast.54, bf16[1152,1152]{1,0:T(8,128)(2,1)} %param.17, bf16[1152,1024]{0,1:T(8,128)(2,1)} %copy.32, ...), kind=kOutput, calls=%fused_computation.57 | convolution fusion | flops 5446434816 | bytes 14755456 | tf_op jit(solution)/shard_map/dot_general | solution.py:42
  87.1 6.8 %copy.34 = bf16[1152,2,512]{2,1,0:T(2,128)(2,1)} copy(bf16[1152,2,512]{0,2,1:T(8,128)(2,1)} %bitcast.56) | data formatting | bytes 4718592 | tf_op jit(solution)/shard_map/reshape | solution.py:46
  93.9 5.8 %all-to-all-start.1 = ((bf16[1152,2,512]{2,1,0:T(2,128)(2,1)}), bf16[1152,2,512]{2,1,0:T(2,128)(2,1)}, u32[]{:S(2)}, u32[]{:S(2)}) async-start(bf16[1152,2,512]{2,1,0:T(2,128)(2,1)} %copy.34), calls=%async_computation.1 | async-start | bytes 4718592 | tf_op jit(solution)/shard_map/all_to_all | solution.py:87
  100.5 27.2 %all-to-all-done.1 = bf16[1152,2,512]{2,1,0:T(2,128)(2,1)} async-done(((bf16[1152,2,512]{2,1,0:T(2,128)(2,1)}), bf16[1152,2,512]{2,1,0:T(2,128)(2,1)}, u32[]{:S(2)}, u32[]{:S(2)}) %all-to-all-start.1) | async-done | bytes 2359328 | tf_op jit(solution)/shard_map/all_to_all | solution.py:87
  140.1 3.3 %collective-permute-done.1 = f32[144,1,512]{2,0,1:T(8,128)S(1)} collective-permute-done((f32[144,1,512]{2,0,1:T(8,128)S(1)}, f32[144,1,512]{2,0,1:T(8,128)S(1)}, u32[]{:S(2)}, u32[]{:S(2)}) %collective-permute-start.1) | collective-permute-done | bytes 294944 | tf_op jit(solution)/shard_map/ppermute | solution.py:19
  143.4 4.1 %collective-permute-done = f32[144,1,512]{2,0,1:T(8,128)S(1)} collective-permute-done((f32[144,1,512]{2,0,1:T(8,128)S(1)}, f32[144,1,512]{2,0,1:T(8,128)S(1)}, u32[]{:S(2)}, u32[]{:S(2)}) %collective-permute-start) | collective-permute-done | bytes 294944 | tf_op jit(solution)/shard_map/ppermute | solution.py:16
  155.2 3.6 %fusion.4 = f32[144,16,513]{2,0,1:T(8,128)} fusion(f32[144,16,512]{2,0,1:T(8,128)S(1)} %fusion.27, f32[144]{0:T(256)S(1)} %bitcast.72, f32[144]{0:T(256)S(1)} %bitcast.68), kind=kLoop, calls=%fused_computation.14 | loop fusion | flops 3545856 | bytes 9447552 | tf_op jit(solution)/shard_map/add | solution.py:58
  159.2 4.1 %collective-permute-done.2 = f32[144,1,512]{2,0,1:T(8,128)S(1)} collective-permute-done((f32[144,1,512]{2,0,1:T(8,128)S(1)}, f32[144,1,512]{2,0,1:T(8,128)S(1)}, u32[]{:S(2)}, u32[]{:S(2)}) %collective-permute-start.2) | collective-permute-done | bytes 294944 | tf_op jit(solution)/shard_map/ppermute | solution.py:16
  164.9 5.5 %fusion.24 = f32[144,16,512]{2,0,1:T(8,128)S(1)} fusion(f32[144,17,512]{2,0,1:T(8,128)S(1)} %fusion.13, f32[144,16,512]{2,0,1:T(8,128)S(1)} %fusion.27, f32[144,16,513]{2,0,1:T(8,128)} %fusion.4, f32[16,512]{1,0:T(8,128)S(1)} %convert_element_type.57), kind=kLoop, calls=%fused_computation.47 | loop fusion | flops 5898240 | bytes 28344320 | tf_op jit(solution)/shard_map/mul | solution.py:61
  170.4 2.5 %collective-permute-start.5 = (f32[144,1,512]{2,0,1:T(8,128)S(1)}, f32[144,1,512]{2,0,1:T(8,128)S(1)}, u32[]{:S(2)}, u32[]{:S(2)}) collective-permute-start(f32[144,1,512]{2,0,1:T(8,128)S(1)} %get-tuple-element.9), channel_id=1, source_target_pairs={{1,0},{2,1},{3,2},{5,4},{6,5},{7,6},{9,8},{10,9},{11,10},{13,12},{... | collective-permute-start | bytes 884744 | tf_op jit(solution)/shard_map/ppermute | solution.py:19
  174.5 3.6 %fusion.7 = f32[144,16,513]{2,0,1:T(8,128)} fusion(f32[144,16,512]{2,0,1:T(8,128)S(1)} %fusion.24, f32[144]{0:T(256)S(1)} %bitcast.73, f32[144]{0:T(256)S(1)} %bitcast.69), kind=kLoop, calls=%fused_computation.17 | loop fusion | flops 3545856 | bytes 9447552 | tf_op jit(solution)/shard_map/add | solution.py:58
  178.1 3.5 %collective-permute-done.4 = f32[144,1,512]{2,0,1:T(8,128)S(1)} collective-permute-done((f32[144,1,512]{2,0,1:T(8,128)S(1)}, f32[144,1,512]{2,0,1:T(8,128)S(1)}, u32[]{:S(2)}, u32[]{:S(2)}) %collective-permute-start.4) | collective-permute-done | bytes 294944 | tf_op jit(solution)/shard_map/ppermute | solution.py:16
  183.1 5.5 %fusion.21 = f32[144,16,512]{2,0,1:T(8,128)S(1)} fusion(f32[144,17,512]{2,0,1:T(8,128)S(1)} %fusion.14, f32[144,16,512]{2,0,1:T(8,128)S(1)} %fusion.24, f32[144,16,513]{2,0,1:T(8,128)} %fusion.7, f32[16,512]{1,0:T(8,128)S(1)} %convert_element_type.57), kind=kLoop, calls=%fused_computation.42 | loop fusion | flops 5898240 | bytes 28344320 | tf_op jit(solution)/shard_map/mul | solution.py:61
  188.7 2.4 %collective-permute-start.7 = (f32[144,1,512]{2,0,1:T(8,128)S(1)}, f32[144,1,512]{2,0,1:T(8,128)S(1)}, u32[]{:S(2)}, u32[]{:S(2)}) collective-permute-start(f32[144,1,512]{2,0,1:T(8,128)S(1)} %get-tuple-element.7), channel_id=1, source_target_pairs={{1,0},{2,1},{3,2},{5,4},{6,5},{7,6},{9,8},{10,9},{11,10},{13,12},{... | collective-permute-start | bytes 884744 | tf_op jit(solution)/shard_map/ppermute | solution.py:19
  195.4 4.4 %collective-permute-done.6 = f32[144,1,512]{2,0,1:T(8,128)S(1)} collective-permute-done((f32[144,1,512]{2,0,1:T(8,128)S(1)}, f32[144,1,512]{2,0,1:T(8,128)S(1)}, u32[]{:S(2)}, u32[]{:S(2)}) %collective-permute-start.6) | collective-permute-done | bytes 294944 | tf_op jit(solution)/shard_map/ppermute | solution.py:16
  201.3 2.5 %fusion.18 = f32[144,16,512]{2,0,1:T(8,128)S(1)} fusion(f32[144,17,512]{2,0,1:T(8,128)S(1)} %fusion.15, f32[144,16,512]{2,0,1:T(8,128)S(1)} %fusion.21, f32[144,16,513]{2,0,1:T(8,128)S(1)} %fusion.10, f32[16,512]{1,0:T(8,128)S(1)} %convert_element_type.57), kind=kLoop, calls=%fused_computation.37 | loop fusion | flops 5898240 | bytes 28344320 | tf_op jit(solution)/shard_map/mul | solution.py:61
  203.8 4.9 %copy.37 = f32[144,16,512]{2,1,0:T(8,128)} copy(f32[144,16,512]{2,0,1:T(8,128)S(1)} %fusion.18) | data formatting | bytes 9437184 | tf_op jit(solution)/shard_map/mul | solution.py:61
  (73 shorter events, 49.7 us)
Async XLA Ops:
  0.0 75.7 %copy-start = (bf16[1152,1152]{1,0:T(8,128)(2,1)S(1)}, bf16[1152,1152]{1,0:T(8,128)(2,1)}, u32[]{:S(2)}) copy-start(bf16[1152,1152]{1,0:T(8,128)(2,1)} %param.18) | copy-start | bytes 7962628
  0.0 23.0 %copy-start.3 = (s32[1152]{0:T(1024)S(1)}, s32[1152]{0:T(1024)}, u32[]{:S(2)}) copy-start(s32[1152]{0:T(1024)} %param.19) | copy-start | bytes 13828
  18.2 32.9 %all-to-all-start = ((bf16[8,144,2,512]{3,2,1,0:T(2,128)(2,1)}), bf16[8,144,2,512]{3,2,1,0:T(2,128)(2,1)}, u32[]{:S(2)}, u32[]{:S(2)}) async-start(bf16[8,144,2,512]{3,2,1,0:T(2,128)(2,1)} %bitcast_dynamic-update-slice_fusion), calls=%async_computation | async-start | bytes 4718592 | tf_op jit(solution)/shard_map/all_to_all | solution.py:90
  71.3 4.4 %copy-start.11 = (f32[1152]{0:T(1024)S(1)}, f32[1152]{0:T(1024)}, u32[]{:S(2)}) copy-start(f32[1152]{0:T(1024)} %param.16) | copy-start | bytes 13828
  87.0 12.6 %copy-start.4 = (s32[16,512]{1,0:T(8,128)S(1)}, s32[16,512]{1,0:T(8,128)}, u32[]{:S(2)}) copy-start(s32[16,512]{1,0:T(8,128)} %param.23) | copy-start | bytes 98308
  87.0 12.7 %copy-start.10 = (f32[8,2]{0,1:T(2,128)S(1)}, f32[8,2]{0,1:T(2,128)}, u32[]{:S(2)}) copy-start(f32[8,2]{0,1:T(2,128)} %param.20) | copy-start | bytes 196
  87.0 12.7 %copy-start.6 = (s32[8,32]{1,0:T(8,128)S(1)}, s32[8,32]{1,0:T(8,128)}, u32[]{:S(2)}) copy-start(s32[8,32]{1,0:T(8,128)} %param.21) | copy-start | bytes 3076
  87.0 12.8 %copy-start.5 = (s32[8,32]{1,0:T(8,128)S(1)}, s32[8,32]{1,0:T(8,128)}, u32[]{:S(2)}) copy-start(s32[8,32]{1,0:T(8,128)} %param.22) | copy-start | bytes 3076
  87.0 13.4 %copy-start.9 = (f32[144]{0:T(256)S(1)}, f32[144]{0:T(256)}, u32[]{:S(2)}) copy-start(f32[144]{0:T(256)} %param.13) | copy-start | bytes 1732
  87.1 13.4 %copy-start.7 = (f32[144,2]{0,1:T(2,128)S(1)}, f32[144,2]{0,1:T(2,128)}, u32[]{:S(2)}) copy-start(f32[144,2]{0,1:T(2,128)} %param.15) | copy-start | bytes 3460
  93.9 33.8 %all-to-all-start.1 = ((bf16[1152,2,512]{2,1,0:T(2,128)(2,1)}), bf16[1152,2,512]{2,1,0:T(2,128)(2,1)}, u32[]{:S(2)}, u32[]{:S(2)}) async-start(bf16[1152,2,512]{2,1,0:T(2,128)(2,1)} %copy.34), calls=%async_computation.1 | async-start | bytes 4718592 | tf_op jit(solution)/shard_map/all_to_all | solution.py:87
  130.4 1.7 copy-start.2
  130.4 1.7 copy-start.8
  134.5 8.8 %collective-permute-start.1 = (f32[144,1,512]{2,0,1:T(8,128)S(1)}, f32[144,1,512]{2,0,1:T(8,128)S(1)}, u32[]{:S(2)}, u32[]{:S(2)}) collective-permute-start(f32[144,1,512]{2,0,1:T(8,128)S(1)} %get-tuple-element.13), channel_id=1, source_target_pairs={{1,0},{2,1},{3,2},{5,4},{6,5},{7,6},{9,8},{10,9},{11,10},{13,12},{... | collective-permute-start | bytes 884744 | tf_op jit(solution)/shard_map/ppermute | solution.py:19
  136.9 10.6 %collective-permute-start = (f32[144,1,512]{2,0,1:T(8,128)S(1)}, f32[144,1,512]{2,0,1:T(8,128)S(1)}, u32[]{:S(2)}, u32[]{:S(2)}) collective-permute-start(f32[144,1,512]{2,0,1:T(8,128)S(1)} %get-tuple-element.14), channel_id=1, source_target_pairs={{0,1},{1,2},{2,3},{4,5},{5,6},{6,7},{8,9},{9,10},{10,11},{12,13},{... | collective-permute-start | bytes 884744 | tf_op jit(solution)/shard_map/ppermute | solution.py:16
  151.5 7.7 %collective-permute-start.3 = (f32[144,1,512]{2,0,1:T(8,128)S(1)}, f32[144,1,512]{2,0,1:T(8,128)S(1)}, u32[]{:S(2)}, u32[]{:S(2)}) collective-permute-start(f32[144,1,512]{2,0,1:T(8,128)S(1)} %get-tuple-element.11), channel_id=1, source_target_pairs={{1,0},{2,1},{3,2},{5,4},{6,5},{7,6},{9,8},{10,9},{11,10},{13,12},{... | collective-permute-start | bytes 884744 | tf_op jit(solution)/shard_map/ppermute | solution.py:19
  153.9 9.4 %collective-permute-start.2 = (f32[144,1,512]{2,0,1:T(8,128)S(1)}, f32[144,1,512]{2,0,1:T(8,128)S(1)}, u32[]{:S(2)}, u32[]{:S(2)}) collective-permute-start(f32[144,1,512]{2,0,1:T(8,128)S(1)} %get-tuple-element.12), channel_id=1, source_target_pairs={{0,1},{1,2},{2,3},{4,5},{5,6},{6,7},{8,9},{9,10},{10,11},{12,13},{... | collective-permute-start | bytes 884744 | tf_op jit(solution)/shard_map/ppermute | solution.py:16
  170.4 7.7 %collective-permute-start.5 = (f32[144,1,512]{2,0,1:T(8,128)S(1)}, f32[144,1,512]{2,0,1:T(8,128)S(1)}, u32[]{:S(2)}, u32[]{:S(2)}) collective-permute-start(f32[144,1,512]{2,0,1:T(8,128)S(1)} %get-tuple-element.9), channel_id=1, source_target_pairs={{1,0},{2,1},{3,2},{5,4},{6,5},{7,6},{9,8},{10,9},{11,10},{13,12},{... | collective-permute-start | bytes 884744 | tf_op jit(solution)/shard_map/ppermute | solution.py:19
  173.0 8.6 %collective-permute-start.4 = (f32[144,1,512]{2,0,1:T(8,128)S(1)}, f32[144,1,512]{2,0,1:T(8,128)S(1)}, u32[]{:S(2)}, u32[]{:S(2)}) collective-permute-start(f32[144,1,512]{2,0,1:T(8,128)S(1)} %get-tuple-element.10), channel_id=1, source_target_pairs={{0,1},{1,2},{2,3},{4,5},{5,6},{6,7},{8,9},{9,10},{10,11},{12,13},{... | collective-permute-start | bytes 884744 | tf_op jit(solution)/shard_map/ppermute | solution.py:16
  188.7 6.6 %collective-permute-start.7 = (f32[144,1,512]{2,0,1:T(8,128)S(1)}, f32[144,1,512]{2,0,1:T(8,128)S(1)}, u32[]{:S(2)}, u32[]{:S(2)}) collective-permute-start(f32[144,1,512]{2,0,1:T(8,128)S(1)} %get-tuple-element.7), channel_id=1, source_target_pairs={{1,0},{2,1},{3,2},{5,4},{6,5},{7,6},{9,8},{10,9},{11,10},{13,12},{... | collective-permute-start | bytes 884744 | tf_op jit(solution)/shard_map/ppermute | solution.py:19
  191.1 8.6 %collective-permute-start.6 = (f32[144,1,512]{2,0,1:T(8,128)S(1)}, f32[144,1,512]{2,0,1:T(8,128)S(1)}, u32[]{:S(2)}, u32[]{:S(2)}) collective-permute-start(f32[144,1,512]{2,0,1:T(8,128)S(1)} %get-tuple-element.8), channel_id=1, source_target_pairs={{0,1},{1,2},{2,3},{4,5},{5,6},{6,7},{8,9},{9,10},{10,11},{12,13},{... | collective-permute-start | bytes 884744 | tf_op jit(solution)/shard_map/ppermute | solution.py:16
  201.3 7.4 %copy-start.1 = (bf16[1152,1152]{1,0:T(8,128)(2,1)S(1)}, bf16[1152,1152]{1,0:T(8,128)(2,1)}, u32[]{:S(2)}) copy-start(bf16[1152,1152]{1,0:T(8,128)(2,1)} %param.18) | copy-start | bytes 7962628
